TPU v7x, 256 devices: a whole 4x4x8 slice. The times are simulated.
256 devices in a mesh: cube: 8 (over x, core), blk: 32 (over z, y).
Axes of the slice: x: 4, y: 4, z: 8, core: 2. Of those that a mesh axis runs over, the one named last changes fastest.
Arguments:
- right_side: float32 [4, 8, 32, 32, 64], P(None, 'cube', 'blk'), may hold values from -6 to 6
- diag_inverse: float32 [3840, 32768], P('cube', 'blk'), as said below
- panels: float32 [3, 8, 32, 2, 16, 32], P(None, 'cube', 'blk'), may hold values from -1 to 1
- extend_map: int32 [3, 8, 32, 2, 16], P(None, 'cube', 'blk'), may hold values from 0 to 31
Outputs:
- solution: float32 [4, 8, 32, 32, 64], P(None, 'cube', 'blk')
Inputs may be any that keep to these rules, and one draw needn't show every extreme that they name: `extend_map`: each entry names one of the 32 parent rows held by the receiving device. `diag_inverse`: dense real entries.
All inputs are finite; a program needn't handle non-finite values.
Results may differ from a plain program's by a relative error of at most 0.0001.
Values sent between devices are 32-bit elements; how exact they have to be, the bound alone decides.
A program may use at most 64 MiB of HBM per device.

v0:
```python
import jax
import jax.numpy as jnp
from jax import lax
from jax.sharding import PartitionSpec as P


def from_partner(block, axis, apart):
    count = lax.axis_size(axis)
    route = []
    for low in range(count):
        high = low | 1 << apart
        if high != low and high < count:
            route += [(low, high), (high, low)]
    return lax.ppermute(block, axis, route)


def collect_pairs(residual_rows, tree_level, cube_index):
    gathered = residual_rows
    for bit_index in range(tree_level):
        partner_rows = from_partner(gathered, "cube", bit_index)
        lower_side = cube_index // 2**bit_index % 2 == 0
        gathered = jnp.where(
            lower_side,
            jnp.concatenate([gathered, partner_rows], axis=0),
            jnp.concatenate([partner_rows, gathered], axis=0),
        )
    return gathered


def reduce_pairs(partial_value, tree_level, cube_index):
    for bit_index in reversed(range(tree_level)):
        half_rows = partial_value.shape[0] // 2
        lower_rows = partial_value[:half_rows]
        upper_rows = partial_value[half_rows:]
        lower_side = cube_index // 2**bit_index % 2 == 0
        kept_rows = jnp.where(lower_side, lower_rows, upper_rows)
        sent_rows = jnp.where(lower_side, upper_rows, lower_rows)
        partial_value = kept_rows + from_partner(sent_rows, "cube", bit_index)
    return partial_value


def body(right_side, diag_inverse, panels, extend_map):
    highest = lax.Precision.HIGHEST
    levels = right_side.shape[0]
    local_rows = right_side.shape[3]
    columns_k = right_side.shape[4]
    cube_index = lax.axis_index("cube")
    rhs_rows = right_side[:, 0, 0]
    panel_blocks = panels[:, 0, 0]
    row_maps = extend_map[:, 0, 0]
    row_ids = jnp.arange(local_rows, dtype=jnp.int32)
    update = jnp.zeros((local_rows, columns_k), jnp.float32)
    solved = []
    onehots = []
    diag_blocks = []
    for tree_level in range(levels):
        span_rows = 2**tree_level * local_rows
        offset = (2**tree_level - 1) * local_rows
        diag_block = diag_inverse[offset : offset + span_rows]
        diag_blocks.append(diag_block)
        residual_rows = rhs_rows[tree_level] - update
        column = collect_pairs(residual_rows, tree_level, cube_index)

        def term_rows(first_row, row_count, diag_block=diag_block, column=column):
            return jnp.einsum("ir,ik->rk", diag_block, column, precision=highest)

        solved_rows = lax.psum_scatter(
            term_rows(jnp.int32(0), lax.axis_size("blk") * local_rows),
            "blk",
            scatter_dimension=0,
            tiled=True,
        )
        solved.append(solved_rows)
        if tree_level + 1 < levels:
            onehot = (row_maps[tree_level][..., None] == row_ids).astype(jnp.float32)
            onehots.append(onehot)
            upd_rows = jnp.einsum(
                "hmr,rk->hmk", panel_blocks[tree_level], solved_rows, precision=highest
            )
            extended = jnp.einsum("hmt,hmk->htk", onehot, upd_rows, precision=highest)
            update = extended[0] + from_partner(extended[1], "cube", tree_level)
    results = [None] * levels
    parent = None
    for tree_level in reversed(range(levels)):
        span_rows = 2**tree_level * local_rows
        diag_block = diag_blocks[tree_level]
        work_rows = solved[tree_level]
        if parent is not None:
            partner_rows = from_partner(parent, "cube", tree_level)
            parent_pair = jnp.stack([parent, partner_rows], axis=0)
            fetched = jnp.einsum(
                "hmt,htk->hmk", onehots[tree_level], parent_pair, precision=highest
            )
            work_rows = work_rows - jnp.einsum(
                "hmr,hmk->rk", panel_blocks[tree_level], fetched, precision=highest
            )

        def accumulate(running, shard_rows, first_row, diag_block=diag_block):
            return jnp.einsum("ir,rk->ik", diag_block, shard_rows, precision=highest)

        initial = jnp.zeros((span_rows, columns_k), jnp.float32)
        partial_value = accumulate(
            initial, lax.all_gather(work_rows, "blk", axis=0, tiled=True), jnp.int32(0)
        )
        parent = reduce_pairs(partial_value, tree_level, cube_index)
        results[tree_level] = parent
    return jnp.stack(results)[:, None, None]


def solution(mesh):
    placed = (
        P(None, "cube", "blk", None, None),
        P("cube", "blk"),
        P(None, "cube", "blk", None, None, None),
        P(None, "cube", "blk", None, None),
    )
    return jax.shard_map(
        body,
        mesh=mesh,
        in_specs=placed,
        out_specs=P(None, "cube", "blk", None, None),
        check_vma=False,
    )
```

profile of v0, /device:TPU:1, one launch (start us, length us, event | category | flops | bytes accessed | tf_op | source)
XLA Modules:
  0.0 1121.1 jit_solution(12477692200826738122)
XLA Ops:
  6.5 2.9 fusion.15
  9.5 0.7 slice_bitcast_fusion.6
  10.2 212.6 %reduce-scatter.11.cloned.1.call-done = f32[32,64]{1,0:T(8,128)} async-done(((f32[1024,64]{1,0:T(8,128)}), f32[32,64]{1,0:T(8,128)}) %reduce-scatter.11.cloned.1.call-update) | async-done | bytes 8208 | tf_op jit(solution)/shard_map/reduce_scatter | solution.py:67
  222.8 0.9 convolution_bitcast_fusion.12
  223.7 0.3 fusion.59
  224.0 5.9 collective-permute-start
  229.9 0.8 collective-permute-done
  230.7 0.7 fusion.46
  231.5 0.3 collective-permute-start.1
  231.8 0.8 collective-permute-done.1
  232.6 1.4 convolution_bitcast_fusion.2
  234.0 1.0 copy.16
  235.1 205.7 %reduce-scatter.13.cloned.1.call-done = f32[32,64]{1,0:T(8,128)} async-done(((f32[1024,64]{1,0:T(8,128)}), f32[32,64]{1,0:T(8,128)}) %reduce-scatter.13.cloned.1.call-update) | async-done | bytes 8208
  440.8 0.8 convolution_bitcast_fusion.11
  441.7 0.3 fusion.58
  442.0 1.3 collective-permute-start.2
  443.2 1.8 collective-permute-done.2
  445.1 6.9 collective-permute-start.3
  452.0 0.8 collective-permute-done.3
  452.8 1.2 collective-permute-start.4
  454.0 1.6 collective-permute-done.4
  455.6 0.4 convolution_bitcast_fusion
  456.0 1.0 copy.18
  457.1 206.9 %reduce-scatter.15.cloned.1.call-done = f32[32,64]{1,0:T(8,128)} async-done(((f32[1024,64]{1,0:T(8,128)}), f32[32,64]{1,0:T(8,128)}) %reduce-scatter.15.cloned.1.call-update) | async-done | bytes 8208
  664.0 0.8 convolution_bitcast_fusion.10
  664.8 0.3 fusion.57
  665.1 2.8 collective-permute-start.5
  667.9 1.4 collective-permute-done.5
  669.3 7.2 collective-permute-start.6
  676.5 0.8 collective-permute-done.6
  677.4 1.2 collective-permute-start.7
  678.6 1.6 collective-permute-done.7
  680.2 2.8 collective-permute-start.8
  683.0 1.9 collective-permute-done.8
  684.9 0.8 convolution_bitcast_fusion.1
  685.7 1.0 copy.20
  686.7 208.0 %reduce-scatter.17.cloned.1.call-done = f32[32,64]{1,0:T(8,128)} async-done(((f32[1024,64]{1,0:T(8,128)}), f32[32,64]{1,0:T(8,128)}) %reduce-scatter.17.cloned.1.call-update) | async-done | bytes 8208 | tf_op jit(solution)/shard_map/reduce_scatter | solution.py:67
  894.7 35.7 %all_gather.12 = f32[1024,64]{1,0:T(8,128)S(1)} all-gather(f32[32,64]{1,0:T(8,128)} %reduce-scatter.17.cloned.1.call-done), channel_id=1, replica_groups=mesh['cube'=8,'blk'=32] {'blk'}, dimensions={0}, use_global_device_ids=true | all-gather | bytes 270336 | tf_op jit(solution)/shard_map/all_gather | solution.py:103
  930.4 1.0 convolution_bitcast_fusion.3
  931.5 2.8 collective-permute-start.9
  934.3 1.6 collective-permute-done.9
  935.9 1.2 collective-permute-start.10
  937.2 1.6 collective-permute-done.10
  938.9 20.6 %collective-permute-start.11 = (f32[32,64]{0,1:T(8,128)S(1)}, f32[32,64]{0,1:T(8,128)S(1)}, u32[]{:S(2)}, u32[]{:S(2)}) collective-permute-start(f32[32,64]{0,1:T(8,128)S(1)} %slice_select_fusion.3), channel_id=1, source_target_pairs={{0,32},{32,0},{64,96},{96,64},{128,160},{160,128},{192,224},{224,1... | collective-permute-start | bytes 24584 | tf_op jit(solution)/shard_map/ppermute | solution.py:14
  959.5 0.9 collective-permute-done.11
  960.4 2.9 collective-permute-start.12
  963.5 1.5 collective-permute-done.12
  965.5 36.1 %all_gather.13 = f32[1024,64]{1,0:T(8,128)S(1)} all-gather(f32[32,64]{1,0:T(8,128)S(1)} %copy.9), channel_id=1, replica_groups=mesh['cube'=8,'blk'=32] {'blk'}, dimensions={0}, use_global_device_ids=true | all-gather | bytes 270336 | tf_op jit(solution)/shard_map/all_gather | solution.py:103
  1001.6 1.0 convolution_bitcast_fusion.7
  1002.7 1.2 collective-permute-start.13
  1003.9 1.6 collective-permute-done.13
  1005.6 14.2 %collective-permute-start.14 = (f32[32,64]{0,1:T(8,128)S(1)}, f32[32,64]{0,1:T(8,128)S(1)}, u32[]{:S(2)}, u32[]{:S(2)}) collective-permute-start(f32[32,64]{0,1:T(8,128)S(1)} %slice_select_fusion.1), channel_id=1, source_target_pairs={{0,32},{32,0},{64,96},{96,64},{128,160},{160,128},{192,224},{224,1... | collective-permute-start | bytes 24584 | tf_op jit(solution)/shard_map/ppermute | solution.py:14
  1019.9 0.9 collective-permute-done.14
  1020.8 1.2 collective-permute-start.15
  1022.0 1.5 collective-permute-done.15
  1024.1 35.8 %all_gather.14 = f32[1024,64]{1,0:T(8,128)S(1)} all-gather(f32[32,64]{1,0:T(8,128)S(1)} %copy.10), channel_id=1, replica_groups=mesh['cube'=8,'blk'=32] {'blk'}, dimensions={0}, use_global_device_ids=true | all-gather | bytes 270336 | tf_op jit(solution)/shard_map/all_gather | solution.py:103
  1059.9 1.0 convolution_bitcast_fusion.5
  1061.0 13.7 %collective-permute-start.16 = (f32[32,64]{0,1:T(8,128)S(1)}, f32[32,64]{0,1:T(8,128)S(1)}, u32[]{:S(2)}, u32[]{:S(2)}) collective-permute-start(f32[32,64]{0,1:T(8,128)S(1)} %slice_select_fusion), channel_id=1, source_target_pairs={{0,32},{32,0},{64,96},{96,64},{128,160},{160,128},{192,224},{224,1... | collective-permute-start | bytes 24584 | tf_op jit(solution)/shard_map/ppermute | solution.py:14
  1074.7 0.9 collective-permute-done.16
  1075.6 0.4 collective-permute-start.17
  1076.0 0.9 collective-permute-done.17
  1077.3 35.5 %all_gather.15 = f32[1024,64]{1,0:T(8,128)S(1)} all-gather(f32[32,64]{1,0:T(8,128)S(1)} %fusion.2), channel_id=1, replica_groups=mesh['cube'=8,'blk'=32] {'blk'}, dimensions={0}, use_global_device_ids=true | all-gather | bytes 270336 | tf_op jit(solution)/shard_map/all_gather | solution.py:103
  1112.8 1.0 convolution_bitcast_fusion.4
  1113.8 0.7 copy.13
  (51 shorter events, 2.7 us)
Async XLA Ops:
  6.5 438.5 %copy-start.5 = (f32[4,1,1,32,64]{4,3,2,1,0:T(8,128)S(1)}, f32[4,1,1,32,64]{4,3,2,1,0:T(8,128)}, u32[]{:S(2)}) copy-start(f32[4,1,1,32,64]{4,3,2,1,0:T(8,128)} %param.4) | copy-start | bytes 98308
  6.5 449.0 %copy-start = (f32[480,1024]{1,0:T(8,128)S(1)}, f32[480,1024]{1,0:T(8,128)}, u32[]{:S(2)}) copy-start(f32[480,1024]{1,0:T(8,128)} %param.5) | copy-start | bytes 5898244
  6.5 434.3 %copy-start.1 = (f32[3,1,1,2,16,32]{5,4,3,2,1,0:T(8,128)S(1)}, f32[3,1,1,2,16,32]{5,4,3,2,1,0:T(8,128)}, u32[]{:S(2)}) copy-start(f32[3,1,1,2,16,32]{5,4,3,2,1,0:T(8,128)} %param.6) | copy-start | bytes 36868
  6.5 216.3 %reduce-scatter.11.cloned.1.call-start = ((), (), s32[]{:S(2)}) async-start(), calls=%async_computation.4 | async-start | bytes 540672 | tf_op jit(solution)/shard_map/reduce_scatter | solution.py:67
  9.4 431.4 %reduce-scatter.13.cloned.1.call-start = ((), (), s32[]{:S(2)}) async-start(), calls=%async_computation.5 | async-start | bytes 540672
  224.0 6.7 collective-permute-start
  231.5 1.2 collective-permute-start.1
  235.0 428.9 %reduce-scatter.15.cloned.1.call-start = ((), (), s32[]{:S(2)}) async-start(), calls=%async_computation.6 | async-start | bytes 540672
  442.0 3.1 collective-permute-start.2
  445.1 7.7 collective-permute-start.3
  452.8 2.8 collective-permute-start.4
  457.0 437.7 %reduce-scatter.17.cloned.1.call-start = ((), (), s32[]{:S(2)}) async-start(), calls=%async_computation.7 | async-start | bytes 540672 | tf_op jit(solution)/shard_map/reduce_scatter | solution.py:67
  665.1 4.2 collective-permute-start.5
  669.3 8.0 collective-permute-start.6
  677.4 2.8 collective-permute-start.7
  680.2 4.7 collective-permute-start.8
  685.6 277.7 %copy-start.3 = (f32[32,64]{1,0:T(8,128)S(1)}, f32[32,64]{1,0:T(8,128)}, u32[]{:S(2)}) copy-start(f32[32,64]{1,0:T(8,128)} %reduce-scatter.15.cloned.1.call-done) | copy-start | bytes 24580
  930.4 91.5 %copy-start.2 = (f32[32,64]{1,0:T(8,128)S(1)}, f32[32,64]{1,0:T(8,128)}, u32[]{:S(2)}) copy-start(f32[32,64]{1,0:T(8,128)} %reduce-scatter.13.cloned.1.call-done) | copy-start | bytes 24580
  931.5 4.4 collective-permute-start.9
  935.9 2.8 collective-permute-start.10
  938.9 21.5 %collective-permute-start.11 = (f32[32,64]{0,1:T(8,128)S(1)}, f32[32,64]{0,1:T(8,128)S(1)}, u32[]{:S(2)}, u32[]{:S(2)}) collective-permute-start(f32[32,64]{0,1:T(8,128)S(1)} %slice_select_fusion.3), channel_id=1, source_target_pairs={{0,32},{32,0},{64,96},{96,64},{128,160},{160,128},{192,224},{224,1... | collective-permute-start | bytes 24584 | tf_op jit(solution)/shard_map/ppermute | solution.py:14
  960.4 4.5 collective-permute-start.12
  965.5 111.6 %copy-start.4 = (f32[32,64]{1,0:T(8,128)S(1)}, f32[32,64]{1,0:T(8,128)}, u32[]{:S(2)}) copy-start(f32[32,64]{1,0:T(8,128)} %reduce-scatter.11.cloned.1.call-done) | copy-start | bytes 24580
  1002.7 2.8 collective-permute-start.13
  1005.6 15.1 %collective-permute-start.14 = (f32[32,64]{0,1:T(8,128)S(1)}, f32[32,64]{0,1:T(8,128)S(1)}, u32[]{:S(2)}, u32[]{:S(2)}) collective-permute-start(f32[32,64]{0,1:T(8,128)S(1)} %slice_select_fusion.1), channel_id=1, source_target_pairs={{0,32},{32,0},{64,96},{96,64},{128,160},{160,128},{192,224},{224,1... | collective-permute-start | bytes 24584 | tf_op jit(solution)/shard_map/ppermute | solution.py:14
  1020.8 2.8 collective-permute-start.15
  1061.0 14.6 %collective-permute-start.16 = (f32[32,64]{0,1:T(8,128)S(1)}, f32[32,64]{0,1:T(8,128)S(1)}, u32[]{:S(2)}, u32[]{:S(2)}) collective-permute-start(f32[32,64]{0,1:T(8,128)S(1)} %slice_select_fusion), channel_id=1, source_target_pairs={{0,32},{32,0},{64,96},{96,64},{128,160},{160,128},{192,224},{224,1... | collective-permute-start | bytes 24584 | tf_op jit(solution)/shard_map/ppermute | solution.py:14
  1075.6 1.2 collective-permute-start.17
Sparse Core Ops, SparseCore 0:
  11.2 211.5 reduce-scatter.10
  235.2 205.6 reduce-scatter.12
  457.2 206.7 reduce-scatter.14
  686.8 207.8 reduce-scatter.16
where the time goes:
time: 1130 us; the launch traced here: 1120 us
  waiting for transfers between devices  856 us (76%)
  blocking collectives  143 us (13%)
  starting transfers between devices  88 us (8%)
  matrix products  14.2 us (1%)
  between operations  13.3 us (1%)
    reduce_scatter x2, waiting for transfers between devices, body(): lax.psum_scatter(term_rows(jnp.int32(0), lax.axis_size('blk') * local_row...  421 us
    unnamed x6, waiting for transfers between devices  413 us
    all_gather x4, blocking collectives, body(): lax.all_gather(work_rows, 'blk', axis=0, tiled=True)  143 us
    ppermute x18, starting transfers between devices, from_partner(): return lax.ppermute(block, axis, route)  87.9 us
    ppermute x18, waiting for transfers between devices, from_partner(): return lax.ppermute(block, axis, route)  22.8 us
  transfers between devices with their start and end apart: 22, of which 22 were waited for; matrix products, arithmetic and copies ran while one was open for 0% of the time, Pallas kernels for 0%

commit v1 on v0

v1 whole, which is shorter than its diff:
```python
import functools

import jax
import jax.numpy as jnp
from jax import lax
from jax.experimental import pallas as pl
from jax.experimental.pallas import tpu as pltpu
from jax.sharding import PartitionSpec as P

F32 = jnp.float32
BF16 = jnp.bfloat16
LEVELS = 4
ROWS = 32
HALF = 16
K = 64
LANES = 2 * K


def split(value):
    high = value.astype(BF16)
    return high, (value - high.astype(F32)).astype(BF16)


def dot(a, b):
    return jnp.dot(a, b, preferred_element_type=F32)


def dot3(a_high, a_low, b):
    b_high, b_low = split(b)
    return dot(a_high, b_high) + (dot(a_high, b_low) + dot(a_low, b_high))


def exact(a, b):
    return jnp.dot(a, b, precision=lax.Precision.HIGHEST, preferred_element_type=F32)


def pack(rows):
    count = rows.shape[0] // ROWS
    parts = rows.reshape(count, 2, HALF, K)
    return jnp.concatenate([parts[:, 0], parts[:, 1]], axis=-1)


def unpack(packed):
    count = packed.shape[0]
    parts = jnp.stack([packed[:, :, :K], packed[:, :, K:]], axis=1)
    return parts.reshape(count * ROWS, K)


def kernel(
    n_cube,
    n_blk,
    rhs_ref,
    diag_ref,
    panels_ref,
    maps_ref,
    out_ref,
    dt_high,
    dt_low,
    d_high,
    d_low,
    mats,
    mats_t,
    solved,
    part,
    rs_recv,
    gather,
    spread,
    sums_send,
    sums_recv,
    rs_send_sem,
    rs_recv_sem,
    ag_send_sem,
    ag_recv_sem,
    up_send_sem,
    up_recv_sem,
    down_send_sem,
    down_recv_sem,
):
    cube = lax.axis_index("cube")
    blk = lax.axis_index("blk")

    def device(c, b):
        return {"cube": c, "blk": b}

    barrier = pltpu.get_barrier_semaphore()

    def greet_blk(step, carry):
        pl.semaphore_signal(
            barrier, inc=1, device_id=device(cube, lax.rem(blk + step, n_blk)),
            device_id_type=pl.DeviceIdType.MESH,
        )
        return carry

    def greet_cube(step, carry):
        pl.semaphore_signal(
            barrier, inc=1, device_id=device(lax.rem(cube + step, n_cube), blk),
            device_id_type=pl.DeviceIdType.MESH,
        )
        return carry

    lax.fori_loop(1, n_blk, greet_blk, 0)
    lax.fori_loop(1, n_cube, greet_cube, 0)

    def rows_of(level):
        return pl.ds((2**level - 1) * ROWS, 2**level * ROWS)

    def prepare_forward(level):
        high, low = split(diag_ref[rows_of(level), :].T)
        dt_high[level, :, : 2**level * ROWS] = high
        dt_low[level, :, : 2**level * ROWS] = low

    def prepare_backward(level):
        high, low = split(diag_ref[rows_of(level), :])
        d_high[rows_of(level), :] = high
        d_low[rows_of(level), :] = low

    def prepare_maps(level):
        row_ids = lax.broadcasted_iota(jnp.int32, (ROWS, HALF), 0)
        for half in range(2):
            onehot = (row_ids == maps_ref[level, half : half + 1, :]).astype(F32)
            mat = exact(onehot, panels_ref[level, half])
            mats[level, half] = mat
            mats_t[level, half] = mat.T

    def wait_for(ref, sem):
        pltpu.make_async_copy(ref, ref, sem).wait()

    def scatter_start(level):
        def step(i, carry):
            to = lax.rem(blk + i, n_blk)
            pltpu.make_async_remote_copy(
                src_ref=part.at[level, to],
                dst_ref=rs_recv.at[level, blk],
                send_sem=rs_send_sem.at[level],
                recv_sem=rs_recv_sem.at[level],
                device_id=device(cube, to),
                device_id_type=pl.DeviceIdType.MESH,
            ).start()
            return carry

        lax.fori_loop(1, n_blk, step, 0)

    def gather_start(level):
        def step(i, carry):
            to = lax.rem(blk + i, n_blk)
            pltpu.make_async_remote_copy(
                src_ref=gather.at[level, blk],
                dst_ref=gather.at[level, blk],
                send_sem=ag_send_sem.at[level],
                recv_sem=ag_recv_sem.at[level],
                device_id=device(cube, to),
                device_id_type=pl.DeviceIdType.MESH,
            ).start()
            return carry

        lax.fori_loop(1, n_blk, step, 0)

    others = pl.ds(0, n_blk - 1)
    prepare_forward(0)
    entry = rhs_ref[0]
    for level in range(LEVELS):
        width = 2**level
        span = width * ROWS
        products = dot3(dt_high[level, :, :span], dt_low[level, :, :span], entry)
        packed = pack(products)
        part[level] = packed
        if level == 0:
            pl.semaphore_wait(barrier, n_blk + n_cube - 2)
        scatter_start(level)
        rs_recv[level, blk] = part[level, blk]
        if level + 1 < LEVELS:
            prepare_maps(level)
            prepare_forward(level + 1)
        else:
            for other in range(LEVELS):
                prepare_backward(other)
        wait_for(rs_recv.at[level, others], rs_recv_sem.at[level])
        solved_packed = jnp.sum(rs_recv[level], axis=0)
        if level + 1 == LEVELS:
            gather[level, blk] = solved_packed
            break
        solved_rows = unpack(solved_packed[None])
        solved[level] = solved_rows
        reach = 2 * width
        base = cube - lax.rem(cube, reach)
        mine = lax.rem(cube, reach)
        kept = rhs_ref[level + 1] - exact(mats[level, 0], solved_rows)
        given = exact(mats[level, 1], solved_rows)
        spread[level, mine, 0] = pack(kept)[0]
        spread[level, mine, 1] = pack(given)[0]

        def up(i, carry, level=level, base=base, mine=mine, reach=reach):
            pltpu.make_async_remote_copy(
                src_ref=spread.at[level, mine],
                dst_ref=spread.at[level, mine],
                send_sem=up_send_sem.at[level],
                recv_sem=up_recv_sem.at[level],
                device_id=device(base + lax.rem(mine + i, reach), blk),
                device_id_type=pl.DeviceIdType.MESH,
            ).start()
            return carry

        lax.fori_loop(1, reach, up, 0)
        wait_for(spread.at[level, pl.ds(0, reach - 1)], up_recv_sem.at[level])
        entry = unpack(
            jnp.stack(
                [
                    spread[level, p, 0] - spread[level, p ^ width, 1]
                    for p in range(reach)
                ]
            )
        )

    for level in reversed(range(LEVELS)):
        width = 2**level
        gather_start(level)
        wait_for(gather.at[level, others], ag_recv_sem.at[level])
        work = unpack(gather[level])
        products = dot3(d_high[rows_of(level), :], d_low[rows_of(level), :], work)
        if level == 0:
            out_ref[0] = products
            break
        packed = pack(products)
        base = cube - lax.rem(cube, width)
        mine = lax.rem(cube, width)
        for p in range(width):
            sums_send[level - 1, p, 0] = packed[p]
            sums_send[level - 1, p, 1] = packed[p ^ (width // 2)]

        def down(i, carry, level=level, base=base, mine=mine, width=width):
            to = lax.rem(mine + i, width)
            pltpu.make_async_remote_copy(
                src_ref=sums_send.at[level - 1, to],
                dst_ref=sums_recv.at[level - 1, mine],
                send_sem=down_send_sem.at[level - 1],
                recv_sem=down_recv_sem.at[level - 1],
                device_id=device(base + to, blk),
                device_id_type=pl.DeviceIdType.MESH,
            ).start()
            return carry

        lax.fori_loop(1, width, down, 0)
        sums_recv[level - 1, mine] = sums_send[level - 1, mine]
        wait_for(
            sums_recv.at[level - 1, pl.ds(0, width - 1)], down_recv_sem.at[level - 1]
        )
        totals = sums_recv[level - 1, 0]
        for p in range(1, width):
            totals = totals + sums_recv[level - 1, p]
        both = unpack(totals)
        own, sibling = both[:ROWS], both[ROWS:]
        out_ref[level] = own
        left = (
            solved[level - 1]
            - exact(mats_t[level - 1, 0], own)
            - exact(mats_t[level - 1, 1], sibling)
        )
        gather[level - 1, blk] = pack(left)[0]

    for level in range(LEVELS):
        wait_for(part.at[level, others], rs_send_sem.at[level])
        wait_for(gather.at[level, others], ag_send_sem.at[level])
        if level + 1 < LEVELS:
            rest = pl.ds(0, 2 * 2**level - 1)
            wait_for(spread.at[level, rest], up_send_sem.at[level])
            wait_for(sums_send.at[level, rest], down_send_sem.at[level])


def body(n_cube, n_blk, right_side, diag_inverse, panels, extend_map):
    rhs = right_side[:, 0, 0]
    blocks = panels[:, 0, 0]
    maps = extend_map[:, 0, 0]
    rows, columns = diag_inverse.shape
    widest = 2 ** (LEVELS - 1)
    vmem = pl.BlockSpec(memory_space=pltpu.VMEM)
    chunks = pltpu.VMEM((LEVELS, n_blk, HALF, LANES), F32)
    pairs = pltpu.VMEM((LEVELS - 1, widest, 2, HALF, LANES), F32)
    result = pl.pallas_call(
        functools.partial(kernel, n_cube, n_blk),
        out_shape=jax.ShapeDtypeStruct(rhs.shape, F32),
        in_specs=[vmem] * 4,
        out_specs=vmem,
        scratch_shapes=[
            pltpu.VMEM((LEVELS, columns, widest * ROWS), BF16),
            pltpu.VMEM((LEVELS, columns, widest * ROWS), BF16),
            pltpu.VMEM((rows, columns), BF16),
            pltpu.VMEM((rows, columns), BF16),
            pltpu.VMEM((LEVELS - 1, 2, ROWS, ROWS), F32),
            pltpu.VMEM((LEVELS - 1, 2, ROWS, ROWS), F32),
            pltpu.VMEM((LEVELS - 1, ROWS, K), F32),
            chunks,
            chunks,
            chunks,
            pairs,
            pairs,
            pairs,
        ]
        + [pltpu.SemaphoreType.DMA((LEVELS,))] * 4
        + [pltpu.SemaphoreType.DMA((LEVELS - 1,))] * 4,
        compiler_params=pltpu.CompilerParams(
            collective_id=0, has_side_effects=True, vmem_limit_bytes=48 * 2**20
        ),
    )(rhs, diag_inverse, blocks, maps)
    return result[:, None, None]


def solution(mesh):
    placed = (
        P(None, "cube", "blk", None, None),
        P("cube", "blk"),
        P(None, "cube", "blk", None, None, None),
        P(None, "cube", "blk", None, None),
    )
    return jax.shard_map(
        functools.partial(body, mesh.shape["cube"], mesh.shape["blk"]),
        mesh=mesh,
        in_specs=placed,
        out_specs=P(None, "cube", "blk", None, None),
        check_vma=False,
    )
```

time: 1130 us -> 117 us (0.10)
  waiting for transfers between devices: 856 us -> 0 us
  blocking collectives: 143 us -> 0 us
  Pallas kernels: 0 us -> 112 us
  starting transfers between devices: 88 us -> 0 us
  matrix products: 14.2 us -> 0 us
  between operations: 13.3 us -> 0.01 us
    reduce_scatter x2 -> x0, waiting for transfers between devices: 421 us -> none  [body(): lax.psum_scatter(term_rows(jnp.int32(0), lax.axis_size('blk') * local_row...]
    unnamed x6 -> x0, waiting for transfers between devices: 413 us -> none
    all_gather x4 -> x0, blocking collectives: 143 us -> none  [body(): lax.all_gather(work_rows, 'blk', axis=0, tiled=True)]
    pallas_call x0 -> x1, Pallas kernels: none -> 112 us  [body(): pl.pallas_call(functools.partial(kernel, n_cube, n_blk), out_shape=jax.Sh...]
    ppermute x18 -> x0, starting transfers between devices: 87.9 us -> none  [from_partner(): return lax.ppermute(block, axis, route)]
    ppermute x18 -> x0, waiting for transfers between devices: 22.8 us -> none  [from_partner(): return lax.ppermute(block, axis, route)]
    dot_general x20 -> x0, matrix products: 14.2 us -> none  [the longest x4 5.43 us: term_rows(): return jnp.einsum('ir,ik->rk', diag_block, column, precision=highest)]
  transfers between devices with their start and end apart: 22 -> 0, of which waited for: 22 -> 0; matrix products, arithmetic and copies ran while one was open for 0% -> 0% of each run, Pallas kernels for 0% -> 0%
where the time goes in v1:
time: 117 us; the launch traced here: 116 us
  Pallas kernels  112 us (96%)
  local copies, waits for them, and re-layouts  4.5 us (4%)
    pallas_call x1, Pallas kernels, body(): pl.pallas_call(functools.partial(kernel, n_cube, n_blk), out_shape=jax.Sh...  112 us
    unnamed x9, local copies, waits for them, and re-layouts  4.5 us

profile of v1, /device:TPU:1, one launch (start us, length us, event | category | flops | bytes accessed | tf_op | source)
XLA Modules:
  0.0 116.4 jit_solution(538992732592528612)
XLA Ops:
  0.0 0.0 copy-start
  0.0 1.5 %copy-done = f32[480,1024]{1,0:T(8,128)S(1)} copy-done((f32[480,1024]{1,0:T(8,128)S(1)}, f32[480,1024]{1,0:T(8,128)}, u32[]{:S(2)}) %copy-start) | copy-done | bytes 1966104
  1.5 0.0 copy-start.1
  1.5 0.8 copy-done.1
  2.4 0.0 copy-start.2
  2.4 0.8 copy-done.2
  3.2 0.0 copy-start.3
  3.2 0.7 copy-done.3
  3.9 111.9 %shard_map.46 = f32[4,32,64]{2,1,0:T(8,128)S(1)} custom-call(f32[4,32,64]{2,1,0:T(8,128)S(1)} %bitcast.7, f32[480,1024]{1,0:T(8,128)S(1)} %copy-done, f32[3,2,16,32]{3,2,1,0:T(8,128)S(1)} %bitcast.8, s32[3,2,16]{2,1,0:T(2,128)S(1)} %bitcast.9), custom_call_target="tpu_custom_call" | custom-call | tf_op jit(solution)/shard_map/pallas_call | solution.py:278
  115.8 0.6 copy.7
Async XLA Ops:
  0.0 1.5 %copy-start = (f32[480,1024]{1,0:T(8,128)S(1)}, f32[480,1024]{1,0:T(8,128)}, u32[]{:S(2)}) copy-start(f32[480,1024]{1,0:T(8,128)} %diag_ref.1) | copy-start | bytes 5898244
  1.5 0.8 copy-start.1
  2.4 0.8 copy-start.2
  3.2 0.7 copy-start.3

commit v2 on v1

--- a/solution.py
+++ b/solution.py
@@ -14,6 +14,7 @@
 HALF = 16
 K = 64
 LANES = 2 * K
+N_Y = 4
 
 
 def split(value):
@@ -49,11 +50,15 @@
 def kernel(
     n_cube,
     n_blk,
+    rhs_hbm,
+    diag_hbm,
+    panels_hbm,
+    maps_hbm,
+    out_ref,
     rhs_ref,
     diag_ref,
     panels_ref,
     maps_ref,
-    out_ref,
     dt_high,
     dt_low,
     d_high,
@@ -75,12 +80,46 @@
     up_recv_sem,
     down_send_sem,
     down_recv_sem,
+    load_sem,
 ):
     cube = lax.axis_index("cube")
     blk = lax.axis_index("blk")
 
+    n_y = min(N_Y, n_blk)
+    depth = n_blk // n_y
+    plane = blk // n_y
+    column = lax.rem(blk, n_y)
+    ring = sorted(
+        [(dz, dy) for dz in range(depth) for dy in range(n_y) if dz + dy],
+        key=lambda at: -(min(at[0], depth - at[0]) + min(at[1], n_y - at[1])),
+    )
+
+    def peer(place):
+        return lax.rem(plane + place[0], depth) * n_y + lax.rem(column + place[1], n_y)
+
     def device(c, b):
         return {"cube": c, "blk": b}
+
+    def rows_of(level):
+        return pl.ds((2**level - 1) * ROWS, 2**level * ROWS)
+
+    diag_loads = [
+        pltpu.make_async_copy(
+            diag_hbm.at[rows_of(level), :],
+            diag_ref.at[rows_of(level), :],
+            load_sem.at[level],
+        )
+        for level in range(LEVELS)
+    ]
+    rhs_load = pltpu.make_async_copy(rhs_hbm, rhs_ref, load_sem.at[LEVELS])
+    panels_load = pltpu.make_async_copy(panels_hbm, panels_ref, load_sem.at[LEVELS + 1])
+    maps_load = pltpu.make_async_copy(maps_hbm, maps_ref, load_sem.at[LEVELS + 2])
+    diag_loads[0].start()
+    rhs_load.start()
+    panels_load.start()
+    maps_load.start()
+    for load in diag_loads[1:]:
+        load.start()
 
     barrier = pltpu.get_barrier_semaphore()
 
@@ -101,10 +140,8 @@
     lax.fori_loop(1, n_blk, greet_blk, 0)
     lax.fori_loop(1, n_cube, greet_cube, 0)
 
-    def rows_of(level):
-        return pl.ds((2**level - 1) * ROWS, 2**level * ROWS)
-
     def prepare_forward(level):
+        diag_loads[level].wait()
         high, low = split(diag_ref[rows_of(level), :].T)
         dt_high[level, :, : 2**level * ROWS] = high
         dt_low[level, :, : 2**level * ROWS] = low
@@ -126,8 +163,8 @@
         pltpu.make_async_copy(ref, ref, sem).wait()
 
     def scatter_start(level):
-        def step(i, carry):
-            to = lax.rem(blk + i, n_blk)
+        def step(place):
+            to = peer(place)
             pltpu.make_async_remote_copy(
                 src_ref=part.at[level, to],
                 dst_ref=rs_recv.at[level, blk],
@@ -136,13 +173,13 @@
                 device_id=device(cube, to),
                 device_id_type=pl.DeviceIdType.MESH,
             ).start()
-            return carry
-
-        lax.fori_loop(1, n_blk, step, 0)
+
+        for place in ring:
+            step(place)
 
     def gather_start(level):
-        def step(i, carry):
-            to = lax.rem(blk + i, n_blk)
+        def step(place):
+            to = peer(place)
             pltpu.make_async_remote_copy(
                 src_ref=gather.at[level, blk],
                 dst_ref=gather.at[level, blk],
@@ -151,12 +188,13 @@
                 device_id=device(cube, to),
                 device_id_type=pl.DeviceIdType.MESH,
             ).start()
-            return carry
-
-        lax.fori_loop(1, n_blk, step, 0)
+
+        for place in ring:
+            step(place)
 
     others = pl.ds(0, n_blk - 1)
     prepare_forward(0)
+    rhs_load.wait()
     entry = rhs_ref[0]
     for level in range(LEVELS):
         width = 2**level
@@ -168,6 +206,9 @@
             pl.semaphore_wait(barrier, n_blk + n_cube - 2)
         scatter_start(level)
         rs_recv[level, blk] = part[level, blk]
+        if level == 0:
+            panels_load.wait()
+            maps_load.wait()
         if level + 1 < LEVELS:
             prepare_maps(level)
             prepare_forward(level + 1)
@@ -278,9 +319,13 @@
     result = pl.pallas_call(
         functools.partial(kernel, n_cube, n_blk),
         out_shape=jax.ShapeDtypeStruct(rhs.shape, F32),
-        in_specs=[vmem] * 4,
+        in_specs=[pl.BlockSpec(memory_space=pltpu.HBM)] * 4,
         out_specs=vmem,
         scratch_shapes=[
+            pltpu.VMEM(rhs.shape, F32),
+            pltpu.VMEM(diag_inverse.shape, F32),
+            pltpu.VMEM(blocks.shape, F32),
+            pltpu.VMEM(maps.shape, jnp.int32),
             pltpu.VMEM((LEVELS, columns, widest * ROWS), BF16),
             pltpu.VMEM((LEVELS, columns, widest * ROWS), BF16),
             pltpu.VMEM((rows, columns), BF16),
@@ -296,9 +341,10 @@
             pairs,
         ]
         + [pltpu.SemaphoreType.DMA((LEVELS,))] * 4
-        + [pltpu.SemaphoreType.DMA((LEVELS - 1,))] * 4,
+        + [pltpu.SemaphoreType.DMA((LEVELS - 1,))] * 4
+        + [pltpu.SemaphoreType.DMA((LEVELS + 3,))],
         compiler_params=pltpu.CompilerParams(
-            collective_id=0, has_side_effects=True, vmem_limit_bytes=48 * 2**20
+            collective_id=0, has_side_effects=True, vmem_limit_bytes=62 * 2**20
         ),
     )(rhs, diag_inverse, blocks, maps)
     return result[:, None, None]

time: 117 us -> 104 us (0.89)
  Pallas kernels: 112 us -> 103 us
  local copies, waits for them, and re-layouts: 4.5 us -> 1.47 us
    pallas_call x1, Pallas kernels: 112 us -> 103 us  [body(): pl.pallas_call(functools.partial(kernel, n_cube, n_blk), out_shape=jax.Sh...]
    unnamed x9 -> x1, local copies, waits for them, and re-layouts: 4.5 us -> 1.47 us
where the time goes in v2:
time: 104 us
  Pallas kernels  103 us (99%)
  local copies, waits for them, and re-layouts  1.47 us (1%)
    pallas_call x1, Pallas kernels, body(): pl.pallas_call(functools.partial(kernel, n_cube, n_blk), out_shape=jax.Sh...  103 us

profile of v2, /device:TPU:1, one launch (start us, length us, event | category | flops | bytes accessed | tf_op | source)
XLA Modules:
  0.0 104.3 jit_solution(10751826112139408084)
XLA Ops:
  0.0 102.8 %shard_map.46 = f32[4,32,64]{2,1,0:T(8,128)} custom-call(f32[4,32,64]{2,1,0:T(8,128)} %bitcast.7, f32[480,1024]{1,0:T(8,128)} %diag_hbm.1, f32[3,2,16,32]{3,2,1,0:T(8,128)} %bitcast.8, s32[3,2,16]{2,1,0:T(2,128)} %bitcast.9), custom_call_target="tpu_custom_call" | custom-call | tf_op jit(solution)/shard_map/pallas_call | solution.py:319
  102.8 1.5 %copy.7 = f32[4,1,1,32,64]{4,3,2,1,0:T(8,128)} copy(f32[4,1,1,32,64]{4,3,2,1,0:T(8,128)} %bitcast.6) | data formatting | bytes 65536

commit v3 on v2

v3 whole, which is shorter than its diff:
```python
import functools

import jax
import jax.numpy as jnp
from jax import lax
from jax.experimental import pallas as pl
from jax.experimental.pallas import tpu as pltpu
from jax.sharding import PartitionSpec as P

F32 = jnp.float32
BF16 = jnp.bfloat16
LEVELS = 4
ROWS = 32
MAPPED = 16
K = 64
STREAMS = 2
COLS = K // STREAMS
LANES = 128
FOLD = LANES // COLS
SUB = ROWS // FOLD
N_Y = 4


def split(value):
    high = value.astype(BF16)
    return high, (value - high.astype(F32)).astype(BF16)


def dot(a, b):
    return jnp.dot(a, b, preferred_element_type=F32)


def dot3(a_high, a_low, b):
    b_high, b_low = split(b)
    wide = dot(a_high, jnp.concatenate([b_high, b_low], axis=1))
    return wide[:, :COLS] + (wide[:, COLS:] + dot(a_low, b_high))


def exact(a, b):
    return jnp.dot(a, b, precision=lax.Precision.HIGHEST, preferred_element_type=F32)


def pack(rows):
    count = rows.shape[0] // ROWS
    parts = rows.reshape(count, FOLD, SUB, COLS)
    return jnp.concatenate([parts[:, i] for i in range(FOLD)], axis=-1)


def unpack(packed):
    count = packed.shape[0]
    parts = [packed[:, :, i * COLS : (i + 1) * COLS] for i in range(FOLD)]
    return jnp.stack(parts, axis=1).reshape(count * ROWS, COLS)


def kernel(
    n_cube,
    n_blk,
    rhs_hbm,
    diag_hbm,
    panels_hbm,
    maps_hbm,
    out_ref,
    rhs_ref,
    diag_ref,
    panels_ref,
    maps_ref,
    dt_high,
    dt_low,
    d_high,
    d_low,
    mats,
    mats_t,
    solved,
    part,
    rs_recv,
    gather,
    spread,
    sums_send,
    sums_recv,
    rs_send_sem,
    rs_recv_sem,
    ag_send_sem,
    ag_recv_sem,
    up_send_sem,
    up_recv_sem,
    down_send_sem,
    down_recv_sem,
    load_sem,
):
    cube = lax.axis_index("cube")
    blk = lax.axis_index("blk")

    n_y = min(N_Y, n_blk)
    depth = n_blk // n_y
    plane = blk // n_y
    column = lax.rem(blk, n_y)
    ring = sorted(
        [(dz, dy) for dz in range(depth) for dy in range(n_y) if dz + dy],
        key=lambda at: -(min(at[0], depth - at[0]) + min(at[1], n_y - at[1])),
    )

    def peer(place):
        return lax.rem(plane + place[0], depth) * n_y + lax.rem(column + place[1], n_y)

    def device(c, b):
        return {"cube": c, "blk": b}

    def rows_of(level):
        return pl.ds((2**level - 1) * ROWS, 2**level * ROWS)

    diag_loads = [
        pltpu.make_async_copy(
            diag_hbm.at[rows_of(level), :],
            diag_ref.at[rows_of(level), :],
            load_sem.at[level],
        )
        for level in range(LEVELS)
    ]
    rhs_load = pltpu.make_async_copy(rhs_hbm, rhs_ref, load_sem.at[LEVELS])
    panels_load = pltpu.make_async_copy(panels_hbm, panels_ref, load_sem.at[LEVELS + 1])
    maps_load = pltpu.make_async_copy(maps_hbm, maps_ref, load_sem.at[LEVELS + 2])
    diag_loads[0].start()
    rhs_load.start()
    panels_load.start()
    maps_load.start()
    for load in diag_loads[1:]:
        load.start()

    barrier = pltpu.get_barrier_semaphore()

    def greet_blk(step, carry):
        pl.semaphore_signal(
            barrier, inc=1, device_id=device(cube, lax.rem(blk + step, n_blk)),
            device_id_type=pl.DeviceIdType.MESH,
        )
        return carry

    def greet_cube(step, carry):
        pl.semaphore_signal(
            barrier, inc=1, device_id=device(lax.rem(cube + step, n_cube), blk),
            device_id_type=pl.DeviceIdType.MESH,
        )
        return carry

    lax.fori_loop(1, n_blk, greet_blk, 0)
    lax.fori_loop(1, n_cube, greet_cube, 0)

    def prepare_forward(level):
        diag_loads[level].wait()
        high, low = split(diag_ref[rows_of(level), :].T)
        dt_high[level, :, : 2**level * ROWS] = high
        dt_low[level, :, : 2**level * ROWS] = low

    def prepare_backward(level):
        high, low = split(diag_ref[rows_of(level), :])
        d_high[rows_of(level), :] = high
        d_low[rows_of(level), :] = low

    def prepare_maps(level):
        row_ids = lax.broadcasted_iota(jnp.int32, (ROWS, MAPPED), 0)
        for half in range(2):
            onehot = (row_ids == maps_ref[level, half : half + 1, :]).astype(F32)
            mat = exact(onehot, panels_ref[level, half])
            mats[level, half] = mat
            mats_t[level, half] = mat.T

    def wait_for(ref, sem):
        pltpu.make_async_copy(ref, ref, sem).wait()

    def scatter_start(stream, level):
        def step(place):
            to = peer(place)
            pltpu.make_async_remote_copy(
                src_ref=part.at[stream, level, to],
                dst_ref=rs_recv.at[stream, level, blk],
                send_sem=rs_send_sem.at[stream, level],
                recv_sem=rs_recv_sem.at[stream, level],
                device_id=device(cube, to),
                device_id_type=pl.DeviceIdType.MESH,
            ).start()

        for place in ring:
            step(place)

    def gather_start(stream, level):
        def step(place):
            to = peer(place)
            pltpu.make_async_remote_copy(
                src_ref=gather.at[stream, level, blk],
                dst_ref=gather.at[stream, level, blk],
                send_sem=ag_send_sem.at[stream, level],
                recv_sem=ag_recv_sem.at[stream, level],
                device_id=device(cube, to),
                device_id_type=pl.DeviceIdType.MESH,
            ).start()

        for place in ring:
            step(place)

    others = pl.ds(0, n_blk - 1)
    streams = range(STREAMS)

    def columns_of(stream):
        return pl.ds(stream * COLS, COLS)

    def scatter(stream, level, entry):
        span = 2**level * ROWS
        products = dot3(dt_high[level, :, :span], dt_low[level, :, :span], entry)
        part[stream, level] = pack(products)
        if level == 0 and stream == 0:
            pl.semaphore_wait(barrier, n_blk + n_cube - 2)
        scatter_start(stream, level)
        rs_recv[stream, level, blk] = part[stream, level, blk]

    def climb(stream, level):
        wait_for(rs_recv.at[stream, level, others], rs_recv_sem.at[stream, level])
        solved_packed = jnp.sum(rs_recv[stream, level], axis=0)
        if level + 1 == LEVELS:
            gather[stream, level, blk] = solved_packed
            gather_start(stream, level)
            return
        solved_rows = unpack(solved_packed[None])
        solved[stream, level] = solved_rows
        width = 2**level
        reach = 2 * width
        base = cube - lax.rem(cube, reach)
        mine = lax.rem(cube, reach)
        kept = rhs_ref[level + 1, :, columns_of(stream)] - exact(mats[level, 0], solved_rows)
        given = exact(mats[level, 1], solved_rows)
        spread[stream, level, mine, 0] = pack(kept)[0]
        spread[stream, level, mine, 1] = pack(given)[0]

        def up(i, carry):
            pltpu.make_async_remote_copy(
                src_ref=spread.at[stream, level, mine],
                dst_ref=spread.at[stream, level, mine],
                send_sem=up_send_sem.at[stream, level],
                recv_sem=up_recv_sem.at[stream, level],
                device_id=device(base + lax.rem(mine + i, reach), blk),
                device_id_type=pl.DeviceIdType.MESH,
            ).start()
            return carry

        lax.fori_loop(1, reach, up, 0)
        wait_for(
            spread.at[stream, level, pl.ds(0, reach - 1)], up_recv_sem.at[stream, level]
        )
        entry = [
            spread[stream, level, p, 0] - spread[stream, level, p ^ width, 1]
            for p in range(reach)
        ]
        scatter(stream, level + 1, unpack(jnp.stack(entry)))

    def descend(stream, level):
        wait_for(gather.at[stream, level, others], ag_recv_sem.at[stream, level])
        work = unpack(gather[stream, level])
        products = dot3(d_high[rows_of(level), :], d_low[rows_of(level), :], work)
        if level == 0:
            out_ref[0, :, columns_of(stream)] = products
            return
        packed = pack(products)
        width = 2**level
        base = cube - lax.rem(cube, width)
        mine = lax.rem(cube, width)
        under = level - 1
        for p in range(width):
            sums_send[stream, under, p, 0] = packed[p]
            sums_send[stream, under, p, 1] = packed[p ^ (width // 2)]

        def down(i, carry):
            to = lax.rem(mine + i, width)
            pltpu.make_async_remote_copy(
                src_ref=sums_send.at[stream, under, to],
                dst_ref=sums_recv.at[stream, under, mine],
                send_sem=down_send_sem.at[stream, under],
                recv_sem=down_recv_sem.at[stream, under],
                device_id=device(base + to, blk),
                device_id_type=pl.DeviceIdType.MESH,
            ).start()
            return carry

        lax.fori_loop(1, width, down, 0)
        sums_recv[stream, under, mine] = sums_send[stream, under, mine]
        wait_for(
            sums_recv.at[stream, under, pl.ds(0, width - 1)],
            down_recv_sem.at[stream, under],
        )
        totals = sums_recv[stream, under, 0]
        for p in range(1, width):
            totals = totals + sums_recv[stream, under, p]
        both = unpack(totals)
        own, sibling = both[:ROWS], both[ROWS:]
        left = (
            solved[stream, under]
            - exact(mats_t[under, 0], own)
            - exact(mats_t[under, 1], sibling)
        )
        gather[stream, under, blk] = pack(left)[0]
        gather_start(stream, under)
        out_ref[level, :, columns_of(stream)] = own

    prepare_forward(0)
    rhs_load.wait()
    for stream in streams:
        scatter(stream, 0, rhs_ref[0, :, columns_of(stream)])
    panels_load.wait()
    maps_load.wait()
    for level in range(LEVELS - 1):
        prepare_maps(level)
        prepare_forward(level + 1)
    for level in range(LEVELS):
        prepare_backward(level)
    for level in range(LEVELS):
        for stream in streams:
            climb(stream, level)
    for level in reversed(range(LEVELS)):
        for stream in streams:
            descend(stream, level)

    for stream in streams:
        for level in range(LEVELS):
            wait_for(part.at[stream, level, others], rs_send_sem.at[stream, level])
            wait_for(gather.at[stream, level, others], ag_send_sem.at[stream, level])
            if level + 1 < LEVELS:
                rest = pl.ds(0, 2 * 2**level - 1)
                wait_for(spread.at[stream, level, rest], up_send_sem.at[stream, level])
                wait_for(
                    sums_send.at[stream, level, rest], down_send_sem.at[stream, level]
                )


def body(n_cube, n_blk, right_side, diag_inverse, panels, extend_map):
    rhs = right_side[:, 0, 0]
    blocks = panels[:, 0, 0]
    maps = extend_map[:, 0, 0]
    rows, columns = diag_inverse.shape
    widest = 2 ** (LEVELS - 1)
    vmem = pl.BlockSpec(memory_space=pltpu.VMEM)
    chunks = pltpu.VMEM((STREAMS, LEVELS, n_blk, SUB, LANES), F32)
    pairs = pltpu.VMEM((STREAMS, LEVELS - 1, widest, 2, SUB, LANES), F32)
    result = pl.pallas_call(
        functools.partial(kernel, n_cube, n_blk),
        out_shape=jax.ShapeDtypeStruct(rhs.shape, F32),
        in_specs=[pl.BlockSpec(memory_space=pltpu.HBM)] * 4,
        out_specs=vmem,
        scratch_shapes=[
            pltpu.VMEM(rhs.shape, F32),
            pltpu.VMEM(diag_inverse.shape, F32),
            pltpu.VMEM(blocks.shape, F32),
            pltpu.VMEM(maps.shape, jnp.int32),
            pltpu.VMEM((LEVELS, columns, widest * ROWS), BF16),
            pltpu.VMEM((LEVELS, columns, widest * ROWS), BF16),
            pltpu.VMEM((rows, columns), BF16),
            pltpu.VMEM((rows, columns), BF16),
            pltpu.VMEM((LEVELS - 1, 2, ROWS, ROWS), F32),
            pltpu.VMEM((LEVELS - 1, 2, ROWS, ROWS), F32),
            pltpu.VMEM((STREAMS, LEVELS - 1, ROWS, COLS), F32),
            chunks,
            chunks,
            chunks,
            pairs,
            pairs,
            pairs,
        ]
        + [pltpu.SemaphoreType.DMA((STREAMS, LEVELS))] * 4
        + [pltpu.SemaphoreType.DMA((STREAMS, LEVELS - 1))] * 4
        + [pltpu.SemaphoreType.DMA((LEVELS + 3,))],
        compiler_params=pltpu.CompilerParams(
            collective_id=0, has_side_effects=True, vmem_limit_bytes=62 * 2**20
        ),
    )(rhs, diag_inverse, blocks, maps)
    return result[:, None, None]


def solution(mesh):
    placed = (
        P(None, "cube", "blk", None, None),
        P("cube", "blk"),
        P(None, "cube", "blk", None, None, None),
        P(None, "cube", "blk", None, None),
    )
    return jax.shard_map(
        functools.partial(body, mesh.shape["cube"], mesh.shape["blk"]),
        mesh=mesh,
        in_specs=placed,
        out_specs=P(None, "cube", "blk", None, None),
        check_vma=False,
    )
```

time: 104 us -> 93 us (0.89)
  Pallas kernels: 103 us -> 91.4 us
    pallas_call x1, Pallas kernels: 103 us -> 91.4 us  [body(): pl.pallas_call(functools.partial(kernel, n_cube, n_blk), out_shape=jax.Sh...]
where the time goes in v3:
time: 93 us; the launch traced here: 92.9 us
  Pallas kernels  91.4 us (98%)
  local copies, waits for them, and re-layouts  1.47 us (2%)
    pallas_call x1, Pallas kernels, body(): pl.pallas_call(functools.partial(kernel, n_cube, n_blk), out_shape=jax.Sh...  91.4 us

profile of v3, /device:TPU:1, one launch (start us, length us, event | category | flops | bytes accessed | tf_op | source)
XLA Modules:
  0.0 92.9 jit_solution(6265553025801273271)
XLA Ops:
  0.0 91.4 %shard_map.46 = f32[4,32,64]{2,1,0:T(8,128)} custom-call(f32[4,32,64]{2,1,0:T(8,128)} %bitcast.7, f32[480,1024]{1,0:T(8,128)} %diag_hbm.1, f32[3,2,16,32]{3,2,1,0:T(8,128)} %bitcast.8, s32[3,2,16]{2,1,0:T(2,128)} %bitcast.9), custom_call_target="tpu_custom_call" | custom-call | tf_op jit(solution)/shard_map/pallas_call | solution.py:341
  91.4 1.5 %copy.7 = f32[4,1,1,32,64]{4,3,2,1,0:T(8,128)} copy(f32[4,1,1,32,64]{4,3,2,1,0:T(8,128)} %bitcast.6) | data formatting | bytes 65536

commit v4 on v3

--- a/solution.py
+++ b/solution.py
@@ -19,6 +19,8 @@
 FOLD = LANES // COLS
 SUB = ROWS // FOLD
 N_Y = 4
+UP_TURNS = (False, True, True, False)
+DOWN_TURNS = (False, False, True, True)
 
 
 def split(value):
@@ -30,10 +32,49 @@
     return jnp.dot(a, b, preferred_element_type=F32)
 
 
-def dot3(a_high, a_low, b):
-    b_high, b_low = split(b)
-    wide = dot(a_high, jnp.concatenate([b_high, b_low], axis=1))
-    return wide[:, :COLS] + (wide[:, COLS:] + dot(a_low, b_high))
+def left_terms(value):
+    high, low = split(value)
+    return jnp.concatenate([high, high, low], axis=1)
+
+
+def right_terms(value):
+    high, low = split(value)
+    return jnp.concatenate([high, low, high], axis=0)
+
+
+def lane_group(shape):
+    return lax.broadcasted_iota(jnp.int32, shape, len(shape) - 1) // COLS
+
+
+def spread_terms(packed):
+    count = packed.shape[0]
+    high = packed.astype(BF16).astype(F32)
+    blocks = []
+    for value in (high, packed - high):
+        turned = [value] + [pltpu.roll(value, COLS * i, 2) for i in range(1, FOLD)]
+        block = []
+        for lanes in range(FOLD):
+            rows = [turned[(lanes - fold) % FOLD] for fold in range(FOLD)]
+            rows = jnp.stack(rows, axis=1)
+            rows = jnp.where(lane_group(rows.shape) == lanes, rows, 0.0)
+            block.append(rows.reshape(count * ROWS, LANES))
+        blocks.append(jnp.concatenate(block, axis=0).astype(BF16))
+    return jnp.concatenate([blocks[0], blocks[1], blocks[0]], axis=0)
+
+
+def collect_terms(terms, count):
+    parts = terms.reshape(FOLD, count, FOLD, SUB, LANES)
+    group = lane_group((count, SUB, LANES))
+    total = None
+    for turn in range(FOLD):
+        piece = parts[0, :, turn]
+        for fold in range(1, FOLD):
+            piece = jnp.where(group == fold, parts[fold, :, (fold + turn) % FOLD], piece)
+        if turn:
+            total = total + pltpu.roll(piece, COLS * turn, 2)
+        else:
+            total = piece
+    return total
 
 
 def exact(a, b):
@@ -64,10 +105,8 @@
     diag_ref,
     panels_ref,
     maps_ref,
-    dt_high,
-    dt_low,
-    d_high,
-    d_low,
+    forward,
+    backward,
     mats,
     mats_t,
     solved,
@@ -102,6 +141,17 @@
     def peer(place):
         return lax.rem(plane + place[0], depth) * n_y + lax.rem(column + place[1], n_y)
 
+    def members(mine, size):
+        chips = size // 2
+        order = sorted(
+            [(dx, core) for dx in range(chips) for core in range(2) if dx + core],
+            key=lambda at: -min(at[0], chips - at[0]),
+        )
+        return [
+            lax.rem(mine // 2 + dx, chips) * 2 + lax.rem(lax.rem(mine, 2) + core, 2)
+            for dx, core in order
+        ]
+
     def device(c, b):
         return {"cube": c, "blk": b}
 
@@ -145,24 +195,35 @@
     lax.fori_loop(1, n_blk, greet_blk, 0)
     lax.fori_loop(1, n_cube, greet_cube, 0)
 
+    def wide_of(level):
+        return slice(3 * FOLD * (2**level - 1) * ROWS, 3 * FOLD * (2**(level + 1) - 1) * ROWS)
+
+    def tall_of(level):
+        return slice(FOLD * (2**level - 1) * ROWS, FOLD * (2**(level + 1) - 1) * ROWS)
+
+    def folds_of(level):
+        columns = diag_ref[rows_of(level), :].T
+        span = columns.shape[1]
+        parts = columns.reshape(n_blk, FOLD, SUB, span)
+        return [parts[:, i].reshape(n_blk * SUB, span) for i in range(FOLD)]
+
     def prepare_forward(level):
         diag_loads[level].wait()
-        high, low = split(diag_ref[rows_of(level), :].T)
-        dt_high[level, :, : 2**level * ROWS] = high
-        dt_low[level, :, : 2**level * ROWS] = low
+        terms = left_terms(jnp.concatenate(folds_of(level), axis=1))
+        forward[:, wide_of(level)] = terms
 
     def prepare_backward(level):
-        high, low = split(diag_ref[rows_of(level), :])
-        d_high[rows_of(level), :] = high
-        d_low[rows_of(level), :] = low
+        terms = left_terms(jnp.concatenate([fold.T for fold in folds_of(level)], axis=0))
+        backward[tall_of(level), :] = terms
 
     def prepare_maps(level):
         row_ids = lax.broadcasted_iota(jnp.int32, (ROWS, MAPPED), 0)
+        pair = []
         for half in range(2):
             onehot = (row_ids == maps_ref[level, half : half + 1, :]).astype(F32)
-            mat = exact(onehot, panels_ref[level, half])
-            mats[level, half] = mat
-            mats_t[level, half] = mat.T
+            pair.append(exact(onehot, panels_ref[level, half]))
+        mats[level] = left_terms(jnp.concatenate(pair, axis=0))
+        mats_t[level] = left_terms(jnp.concatenate([mat.T for mat in pair], axis=1))
 
     def wait_for(ref, sem):
         pltpu.make_async_copy(ref, ref, sem).wait()
@@ -204,9 +265,8 @@
         return pl.ds(stream * COLS, COLS)
 
     def scatter(stream, level, entry):
-        span = 2**level * ROWS
-        products = dot3(dt_high[level, :, :span], dt_low[level, :, :span], entry)
-        part[stream, level] = pack(products)
+        products = dot(forward[:, wide_of(level)], spread_terms(entry))
+        part[stream, level] = products.reshape(n_blk, SUB, LANES)
         if level == 0 and stream == 0:
             pl.semaphore_wait(barrier, n_blk + n_cube - 2)
         scatter_start(stream, level)
@@ -225,23 +285,30 @@
         reach = 2 * width
         base = cube - lax.rem(cube, reach)
         mine = lax.rem(cube, reach)
-        kept = rhs_ref[level + 1, :, columns_of(stream)] - exact(mats[level, 0], solved_rows)
-        given = exact(mats[level, 1], solved_rows)
+        updates = dot(mats[level], right_terms(solved_rows))
+        kept = rhs_ref[level + 1, :, columns_of(stream)] - updates[:ROWS]
+        given = updates[ROWS:]
         spread[stream, level, mine, 0] = pack(kept)[0]
         spread[stream, level, mine, 1] = pack(given)[0]
 
-        def up(i, carry):
+        def up(member):
             pltpu.make_async_remote_copy(
                 src_ref=spread.at[stream, level, mine],
                 dst_ref=spread.at[stream, level, mine],
                 send_sem=up_send_sem.at[stream, level],
                 recv_sem=up_recv_sem.at[stream, level],
-                device_id=device(base + lax.rem(mine + i, reach), blk),
+                device_id=device(base + member, blk),
                 device_id_type=pl.DeviceIdType.MESH,
             ).start()
-            return carry
-
-        lax.fori_loop(1, reach, up, 0)
+
+        for member in members(mine, reach):
+            up(member)
+
+    def enter(stream, level):
+        if level + 1 == LEVELS:
+            return
+        width = 2**level
+        reach = 2 * width
         wait_for(
             spread.at[stream, level, pl.ds(0, reach - 1)], up_recv_sem.at[stream, level]
         )
@@ -249,16 +316,17 @@
             spread[stream, level, p, 0] - spread[stream, level, p ^ width, 1]
             for p in range(reach)
         ]
-        scatter(stream, level + 1, unpack(jnp.stack(entry)))
+        scatter(stream, level + 1, jnp.stack(entry))
 
     def descend(stream, level):
         wait_for(gather.at[stream, level, others], ag_recv_sem.at[stream, level])
-        work = unpack(gather[stream, level])
-        products = dot3(d_high[rows_of(level), :], d_low[rows_of(level), :], work)
+        work = gather[stream, level].reshape(n_blk * SUB, LANES)
+        packed = collect_terms(
+            dot(backward[tall_of(level), :], right_terms(work)), 2**level
+        )
         if level == 0:
-            out_ref[0, :, columns_of(stream)] = products
+            out_ref[0, :, columns_of(stream)] = unpack(packed)
             return
-        packed = pack(products)
         width = 2**level
         base = cube - lax.rem(cube, width)
         mine = lax.rem(cube, width)
@@ -267,8 +335,7 @@
             sums_send[stream, under, p, 0] = packed[p]
             sums_send[stream, under, p, 1] = packed[p ^ (width // 2)]
 
-        def down(i, carry):
-            to = lax.rem(mine + i, width)
+        def down(to):
             pltpu.make_async_remote_copy(
                 src_ref=sums_send.at[stream, under, to],
                 dst_ref=sums_recv.at[stream, under, mine],
@@ -277,10 +344,16 @@
                 device_id=device(base + to, blk),
                 device_id_type=pl.DeviceIdType.MESH,
             ).start()
-            return carry
-
-        lax.fori_loop(1, width, down, 0)
+
+        for member in members(mine, width):
+            down(member)
         sums_recv[stream, under, mine] = sums_send[stream, under, mine]
+
+    def leave(stream, level):
+        if level == 0:
+            return
+        width = 2**level
+        under = level - 1
         wait_for(
             sums_recv.at[stream, under, pl.ds(0, width - 1)],
             down_recv_sem.at[stream, under],
@@ -289,33 +362,43 @@
         for p in range(1, width):
             totals = totals + sums_recv[stream, under, p]
         both = unpack(totals)
-        own, sibling = both[:ROWS], both[ROWS:]
-        left = (
-            solved[stream, under]
-            - exact(mats_t[under, 0], own)
-            - exact(mats_t[under, 1], sibling)
-        )
+        left = solved[stream, under] - dot(mats_t[under], right_terms(both))
         gather[stream, under, blk] = pack(left)[0]
         gather_start(stream, under)
-        out_ref[level, :, columns_of(stream)] = own
+        out_ref[level, :, columns_of(stream)] = both[:ROWS]
 
     prepare_forward(0)
     rhs_load.wait()
     for stream in streams:
-        scatter(stream, 0, rhs_ref[0, :, columns_of(stream)])
+        scatter(stream, 0, pack(rhs_ref[0, :, columns_of(stream)]))
+    def in_turn(first, second, level, interleave):
+        if interleave:
+            for stream in streams:
+                first(stream, level)
+            for stream in streams:
+                second(stream, level)
+        else:
+            for stream in streams:
+                first(stream, level)
+                second(stream, level)
+
     panels_load.wait()
     maps_load.wait()
-    for level in range(LEVELS - 1):
-        prepare_maps(level)
-        prepare_forward(level + 1)
+    prepare_maps(0)
+    prepare_forward(1)
     for level in range(LEVELS):
-        prepare_backward(level)
-    for level in range(LEVELS):
-        for stream in streams:
-            climb(stream, level)
+        in_turn(climb, enter, level, UP_TURNS[level])
+        if level + 2 < LEVELS:
+            prepare_maps(level + 1)
+            prepare_forward(level + 2)
+        elif level + 2 == LEVELS:
+            prepare_backward(LEVELS - 1)
+            prepare_backward(LEVELS - 2)
+        else:
+            for below in range(LEVELS - 2):
+                prepare_backward(below)
     for level in reversed(range(LEVELS)):
-        for stream in streams:
-            descend(stream, level)
+        in_turn(descend, leave, level, DOWN_TURNS[level])
 
     for stream in streams:
         for level in range(LEVELS):
@@ -348,12 +431,10 @@
             pltpu.VMEM(diag_inverse.shape, F32),
             pltpu.VMEM(blocks.shape, F32),
             pltpu.VMEM(maps.shape, jnp.int32),
-            pltpu.VMEM((LEVELS, columns, widest * ROWS), BF16),
-            pltpu.VMEM((LEVELS, columns, widest * ROWS), BF16),
-            pltpu.VMEM((rows, columns), BF16),
-            pltpu.VMEM((rows, columns), BF16),
-            pltpu.VMEM((LEVELS - 1, 2, ROWS, ROWS), F32),
-            pltpu.VMEM((LEVELS - 1, 2, ROWS, ROWS), F32),
+            pltpu.VMEM((n_blk * SUB, 3 * FOLD * rows), BF16),
+            pltpu.VMEM((FOLD * rows, 3 * n_blk * SUB), BF16),
+            pltpu.VMEM((LEVELS - 1, 2 * ROWS, 3 * ROWS), BF16),
+            pltpu.VMEM((LEVELS - 1, ROWS, 6 * ROWS), BF16),
             pltpu.VMEM((STREAMS, LEVELS - 1, ROWS, COLS), F32),
             chunks,
             chunks,

time: 93 us -> 88.6 us (0.953)
  Pallas kernels: 91.4 us -> 86.9 us
    pallas_call x1, Pallas kernels: 91.4 us -> 86.9 us  [body(): pl.pallas_call(functools.partial(kernel, n_cube, n_blk), out_shape=jax.Sh...]
where the time goes in v4:
time: 88.6 us; the launch traced here: 88.4 us
  Pallas kernels  86.9 us (98%)
  local copies, waits for them, and re-layouts  1.47 us (2%)
    pallas_call x1, Pallas kernels, body(): pl.pallas_call(functools.partial(kernel, n_cube, n_blk), out_shape=jax.Sh...  86.9 us

profile of v4, /device:TPU:1, one launch (start us, length us, event | category | flops | bytes accessed | tf_op | source)
XLA Modules:
  0.0 88.4 jit_solution(8171950217226698065)
XLA Ops:
  0.0 86.9 %shard_map.46 = f32[4,32,64]{2,1,0:T(8,128)} custom-call(f32[4,32,64]{2,1,0:T(8,128)} %bitcast.7, f32[480,1024]{1,0:T(8,128)} %diag_hbm.1, f32[3,2,16,32]{3,2,1,0:T(8,128)} %bitcast.8, s32[3,2,16]{2,1,0:T(2,128)} %bitcast.9), custom_call_target="tpu_custom_call" | custom-call | tf_op jit(solution)/shard_map/pallas_call | solution.py:424
  86.9 1.5 %copy.7 = f32[4,1,1,32,64]{4,3,2,1,0:T(8,128)} copy(f32[4,1,1,32,64]{4,3,2,1,0:T(8,128)} %bitcast.6) | data formatting | bytes 65536

commit v5 on v4

--- a/solution.py
+++ b/solution.py
@@ -19,6 +19,7 @@
 FOLD = LANES // COLS
 SUB = ROWS // FOLD
 N_Y = 4
+SCALE = 32.0
 UP_TURNS = (False, True, True, False)
 DOWN_TURNS = (False, False, True, True)
 
@@ -107,8 +108,9 @@
     maps_ref,
     forward,
     backward,
-    mats,
-    mats_t,
+    correct,
+    base_rows,
+    facts,
     solved,
     part,
     rs_recv,
@@ -116,6 +118,8 @@
     spread,
     sums_send,
     sums_recv,
+    rows_send,
+    rows_recv,
     rs_send_sem,
     rs_recv_sem,
     ag_send_sem,
@@ -124,6 +128,10 @@
     up_recv_sem,
     down_send_sem,
     down_recv_sem,
+    rows_send_sem,
+    rows_recv_sem,
+    fact_send_sem,
+    fact_recv_sem,
     load_sem,
 ):
     cube = lax.axis_index("cube")
@@ -207,23 +215,65 @@
         parts = columns.reshape(n_blk, FOLD, SUB, span)
         return [parts[:, i].reshape(n_blk * SUB, span) for i in range(FOLD)]
 
-    def prepare_forward(level):
-        diag_loads[level].wait()
-        terms = left_terms(jnp.concatenate(folds_of(level), axis=1))
-        forward[:, wide_of(level)] = terms
-
-    def prepare_backward(level):
-        terms = left_terms(jnp.concatenate([fold.T for fold in folds_of(level)], axis=0))
-        backward[tall_of(level), :] = terms
-
-    def prepare_maps(level):
+    def beside(folds):
+        return left_terms(jnp.concatenate(folds, axis=1))
+
+    def below(folds):
+        return left_terms(jnp.concatenate([fold.T for fold in folds], axis=0))
+
+    def prepare_facts(level):
+        reach = 2 * 2**level
+        mine = lax.rem(cube, reach)
         row_ids = lax.broadcasted_iota(jnp.int32, (ROWS, MAPPED), 0)
-        pair = []
         for half in range(2):
             onehot = (row_ids == maps_ref[level, half : half + 1, :]).astype(F32)
-            pair.append(exact(onehot, panels_ref[level, half]))
-        mats[level] = left_terms(jnp.concatenate(pair, axis=0))
-        mats_t[level] = left_terms(jnp.concatenate([mat.T for mat in pair], axis=1))
+            mat = exact(onehot, panels_ref[level, half]) * (-1.0 / SCALE)
+            facts[level, mine, half] = pack(mat)[0]
+        for stream in range(STREAMS):
+            rows = rhs_ref[level + 1, :, columns_of(stream)]
+            facts[level, mine, 2 + stream] = pack(rows)[0]
+
+    def exchange_facts(level):
+        reach = 2 * 2**level
+        base = cube - lax.rem(cube, reach)
+        mine = lax.rem(cube, reach)
+        for member in members(mine, reach):
+            pltpu.make_async_remote_copy(
+                src_ref=facts.at[level, mine],
+                dst_ref=facts.at[level, mine],
+                send_sem=fact_send_sem.at[level],
+                recv_sem=fact_recv_sem.at[level],
+                device_id=device(base + member, blk),
+                device_id_type=pl.DeviceIdType.MESH,
+            ).start()
+
+    def combine(under):
+        level = under + 1
+        width = 2**under
+        reach = 2 * width
+        diag_loads[level].wait()
+        wait_for(facts.at[under, pl.ds(0, reach - 1)], fact_recv_sem.at[under])
+        zero = jnp.zeros((ROWS, ROWS), F32)
+        lines = []
+        for p in range(reach):
+            line = [zero] * reach
+            line[p] = unpack(facts[under, p, 0][None])
+            line[p ^ width] = unpack(facts[under, p ^ width, 1][None])
+            lines.append(jnp.concatenate(line, axis=1))
+        update = jnp.concatenate(lines, axis=0)
+        folds = folds_of(level)
+        stacked = exact(jnp.concatenate(folds, axis=0), update)
+        height = n_blk * SUB
+        merged = [stacked[i * height : (i + 1) * height] for i in range(FOLD)]
+        forward[:, wide_of(level)] = beside(merged)
+        correct[tall_of(level), :] = below(merged)
+        plain = beside(folds)
+        for stream in range(STREAMS):
+            rows = jnp.stack([facts[under, p, 2 + stream] for p in range(reach)])
+            base_rows[stream, under] = dot(plain, spread_terms(rows))
+
+    def prepare_backward(level):
+        backward[tall_of(level), :] = below(folds_of(level))
 
     def wait_for(ref, sem):
         pltpu.make_async_copy(ref, ref, sem).wait()
@@ -266,6 +316,8 @@
 
     def scatter(stream, level, entry):
         products = dot(forward[:, wide_of(level)], spread_terms(entry))
+        if level:
+            products = base_rows[stream, level - 1] + SCALE * products
         part[stream, level] = products.reshape(n_blk, SUB, LANES)
         if level == 0 and stream == 0:
             pl.semaphore_wait(barrier, n_blk + n_cube - 2)
@@ -274,24 +326,16 @@
 
     def climb(stream, level):
         wait_for(rs_recv.at[stream, level, others], rs_recv_sem.at[stream, level])
-        solved_packed = jnp.sum(rs_recv[stream, level], axis=0)
+        rows = jnp.sum(rs_recv[stream, level], axis=0)
         if level + 1 == LEVELS:
-            gather[stream, level, blk] = solved_packed
+            gather[stream, level, blk] = rows
             gather_start(stream, level)
             return
-        solved_rows = unpack(solved_packed[None])
-        solved[stream, level] = solved_rows
-        width = 2**level
-        reach = 2 * width
+        reach = 2 * 2**level
         base = cube - lax.rem(cube, reach)
         mine = lax.rem(cube, reach)
-        updates = dot(mats[level], right_terms(solved_rows))
-        kept = rhs_ref[level + 1, :, columns_of(stream)] - updates[:ROWS]
-        given = updates[ROWS:]
-        spread[stream, level, mine, 0] = pack(kept)[0]
-        spread[stream, level, mine, 1] = pack(given)[0]
-
-        def up(member):
+        spread[stream, level, mine] = rows
+        for member in members(mine, reach):
             pltpu.make_async_remote_copy(
                 src_ref=spread.at[stream, level, mine],
                 dst_ref=spread.at[stream, level, mine],
@@ -300,77 +344,82 @@
                 device_id=device(base + member, blk),
                 device_id_type=pl.DeviceIdType.MESH,
             ).start()
-
-        for member in members(mine, reach):
-            up(member)
+        solved[stream, level] = rows
 
     def enter(stream, level):
         if level + 1 == LEVELS:
             return
-        width = 2**level
-        reach = 2 * width
+        reach = 2 * 2**level
         wait_for(
             spread.at[stream, level, pl.ds(0, reach - 1)], up_recv_sem.at[stream, level]
         )
-        entry = [
-            spread[stream, level, p, 0] - spread[stream, level, p ^ width, 1]
-            for p in range(reach)
-        ]
-        scatter(stream, level + 1, jnp.stack(entry))
-
-    def descend(stream, level):
-        wait_for(gather.at[stream, level, others], ag_recv_sem.at[stream, level])
-        work = gather[stream, level].reshape(n_blk * SUB, LANES)
-        packed = collect_terms(
-            dot(backward[tall_of(level), :], right_terms(work)), 2**level
-        )
-        if level == 0:
-            out_ref[0, :, columns_of(stream)] = unpack(packed)
-            return
+        scatter(stream, level + 1, spread[stream, level, :reach])
+
+    def send_down(stream, level, source, target, send_sem, recv_sem):
         width = 2**level
+        under = level - 1
         base = cube - lax.rem(cube, width)
         mine = lax.rem(cube, width)
-        under = level - 1
-        for p in range(width):
-            sums_send[stream, under, p, 0] = packed[p]
-            sums_send[stream, under, p, 1] = packed[p ^ (width // 2)]
-
-        def down(to):
+        for member in members(mine, width):
             pltpu.make_async_remote_copy(
-                src_ref=sums_send.at[stream, under, to],
-                dst_ref=sums_recv.at[stream, under, mine],
-                send_sem=down_send_sem.at[stream, under],
-                recv_sem=down_recv_sem.at[stream, under],
-                device_id=device(base + to, blk),
+                src_ref=source.at[stream, under, member],
+                dst_ref=target.at[stream, under, mine],
+                send_sem=send_sem.at[stream, under],
+                recv_sem=recv_sem.at[stream, under],
+                device_id=device(base + member, blk),
                 device_id_type=pl.DeviceIdType.MESH,
             ).start()
-
-        for member in members(mine, width):
-            down(member)
-        sums_recv[stream, under, mine] = sums_send[stream, under, mine]
+        target[stream, under, mine] = source[stream, under, mine]
+
+    def receive_down(stream, level, target, recv_sem):
+        width = 2**level
+        under = level - 1
+        wait_for(
+            target.at[stream, under, pl.ds(0, width - 1)], recv_sem.at[stream, under]
+        )
+        return jnp.sum(target[stream, under, :width], axis=0)
+
+    def descend(stream, level):
+        width = 2**level
+        wait_for(gather.at[stream, level, others], ag_recv_sem.at[stream, level])
+        work = right_terms(gather[stream, level].reshape(n_blk * SUB, LANES))
+        if level:
+            sums = collect_terms(dot(correct[tall_of(level), :], work), width)
+            sums_send[stream, level - 1, :width] = sums
+            send_down(stream, level, sums_send, sums_recv, down_send_sem, down_recv_sem)
+        rows = collect_terms(dot(backward[tall_of(level), :], work), width)
+        if level:
+            rows_send[stream, level - 1, :width] = rows
+            send_down(stream, level, rows_send, rows_recv, rows_send_sem, rows_recv_sem)
+        else:
+            out_ref[0, :, columns_of(stream)] = unpack(rows)
 
     def leave(stream, level):
         if level == 0:
             return
-        width = 2**level
         under = level - 1
-        wait_for(
-            sums_recv.at[stream, under, pl.ds(0, width - 1)],
-            down_recv_sem.at[stream, under],
-        )
-        totals = sums_recv[stream, under, 0]
-        for p in range(1, width):
-            totals = totals + sums_recv[stream, under, p]
-        both = unpack(totals)
-        left = solved[stream, under] - dot(mats_t[under], right_terms(both))
-        gather[stream, under, blk] = pack(left)[0]
+        sums = receive_down(stream, level, sums_recv, down_recv_sem)
+        gather[stream, under, blk] = solved[stream, under] + SCALE * sums
         gather_start(stream, under)
-        out_ref[level, :, columns_of(stream)] = both[:ROWS]
-
-    prepare_forward(0)
+
+    def finish(stream, level):
+        if level:
+            rows = receive_down(stream, level, rows_recv, rows_recv_sem)
+            out_ref[level, :, columns_of(stream)] = unpack(rows[None])
+
+    diag_loads[0].wait()
+    forward[:, wide_of(0)] = beside(folds_of(0))
     rhs_load.wait()
     for stream in streams:
         scatter(stream, 0, pack(rhs_ref[0, :, columns_of(stream)]))
+        if stream == 0:
+            panels_load.wait()
+            maps_load.wait()
+            for level in range(LEVELS - 1):
+                prepare_facts(level)
+                exchange_facts(level)
+    combine(0)
+
     def in_turn(first, second, level, interleave):
         if interleave:
             for stream in streams:
@@ -382,24 +431,24 @@
                 first(stream, level)
                 second(stream, level)
 
-    panels_load.wait()
-    maps_load.wait()
-    prepare_maps(0)
-    prepare_forward(1)
     for level in range(LEVELS):
         in_turn(climb, enter, level, UP_TURNS[level])
         if level + 2 < LEVELS:
-            prepare_maps(level + 1)
-            prepare_forward(level + 2)
+            combine(level + 1)
         elif level + 2 == LEVELS:
             prepare_backward(LEVELS - 1)
             prepare_backward(LEVELS - 2)
         else:
-            for below in range(LEVELS - 2):
-                prepare_backward(below)
+            for low in range(LEVELS - 2):
+                prepare_backward(low)
     for level in reversed(range(LEVELS)):
         in_turn(descend, leave, level, DOWN_TURNS[level])
-
+        for stream in streams:
+            finish(stream, level)
+
+    for level in range(LEVELS - 1):
+        rest = pl.ds(0, 2 * 2**level - 1)
+        wait_for(facts.at[level, rest], fact_send_sem.at[level])
     for stream in streams:
         for level in range(LEVELS):
             wait_for(part.at[stream, level, others], rs_send_sem.at[stream, level])
@@ -410,6 +459,9 @@
                 wait_for(
                     sums_send.at[stream, level, rest], down_send_sem.at[stream, level]
                 )
+                wait_for(
+                    rows_send.at[stream, level, rest], rows_send_sem.at[stream, level]
+                )
 
 
 def body(n_cube, n_blk, right_side, diag_inverse, panels, extend_map):
@@ -420,7 +472,7 @@
     widest = 2 ** (LEVELS - 1)
     vmem = pl.BlockSpec(memory_space=pltpu.VMEM)
     chunks = pltpu.VMEM((STREAMS, LEVELS, n_blk, SUB, LANES), F32)
-    pairs = pltpu.VMEM((STREAMS, LEVELS - 1, widest, 2, SUB, LANES), F32)
+    sets = pltpu.VMEM((STREAMS, LEVELS - 1, widest, SUB, LANES), F32)
     result = pl.pallas_call(
         functools.partial(kernel, n_cube, n_blk),
         out_shape=jax.ShapeDtypeStruct(rhs.shape, F32),
@@ -433,18 +485,22 @@
             pltpu.VMEM(maps.shape, jnp.int32),
             pltpu.VMEM((n_blk * SUB, 3 * FOLD * rows), BF16),
             pltpu.VMEM((FOLD * rows, 3 * n_blk * SUB), BF16),
-            pltpu.VMEM((LEVELS - 1, 2 * ROWS, 3 * ROWS), BF16),
-            pltpu.VMEM((LEVELS - 1, ROWS, 6 * ROWS), BF16),
-            pltpu.VMEM((STREAMS, LEVELS - 1, ROWS, COLS), F32),
+            pltpu.VMEM((FOLD * rows, 3 * n_blk * SUB), BF16),
+            pltpu.VMEM((STREAMS, LEVELS - 1, n_blk * SUB, LANES), F32),
+            pltpu.VMEM((LEVELS - 1, widest, 2 + STREAMS, SUB, LANES), F32),
+            pltpu.VMEM((STREAMS, LEVELS - 1, SUB, LANES), F32),
             chunks,
             chunks,
             chunks,
-            pairs,
-            pairs,
-            pairs,
+            sets,
+            sets,
+            sets,
+            sets,
+            sets,
         ]
         + [pltpu.SemaphoreType.DMA((STREAMS, LEVELS))] * 4
-        + [pltpu.SemaphoreType.DMA((STREAMS, LEVELS - 1))] * 4
+        + [pltpu.SemaphoreType.DMA((STREAMS, LEVELS - 1))] * 6
+        + [pltpu.SemaphoreType.DMA((LEVELS - 1,))] * 2
         + [pltpu.SemaphoreType.DMA((LEVELS + 3,))],
         compiler_params=pltpu.CompilerParams(
             collective_id=0, has_side_effects=True, vmem_limit_bytes=62 * 2**20

time: 88.6 us -> 86.6 us (0.977)
  Pallas kernels: 86.9 us -> 85 us
    pallas_call x1, Pallas kernels: 86.9 us -> 85 us  [body(): pl.pallas_call(functools.partial(kernel, n_cube, n_blk), out_shape=jax.Sh...]
where the time goes in v5:
time: 86.6 us; the launch traced here: 86.5 us
  Pallas kernels  85 us (98%)
  local copies, waits for them, and re-layouts  1.47 us (2%)
    pallas_call x1, Pallas kernels, body(): pl.pallas_call(functools.partial(kernel, n_cube, n_blk), out_shape=jax.Sh...  85 us

profile of v5, /device:TPU:1, one launch (start us, length us, event | category | flops | bytes accessed | tf_op | source)
XLA Modules:
  0.0 86.5 jit_solution(4193943646742763033)
XLA Ops:
  0.0 85.0 %shard_map.46 = f32[4,32,64]{2,1,0:T(8,128)} custom-call(f32[4,32,64]{2,1,0:T(8,128)} %bitcast.7, f32[480,1024]{1,0:T(8,128)} %diag_hbm.1, f32[3,2,16,32]{3,2,1,0:T(8,128)} %bitcast.8, s32[3,2,16]{2,1,0:T(2,128)} %bitcast.9), custom_call_target="tpu_custom_call" | custom-call | tf_op jit(solution)/shard_map/pallas_call | solution.py:476
  85.0 1.5 %copy.7 = f32[4,1,1,32,64]{4,3,2,1,0:T(8,128)} copy(f32[4,1,1,32,64]{4,3,2,1,0:T(8,128)} %bitcast.6) | data formatting | bytes 65536

commit v6 on v5

--- a/solution.py
+++ b/solution.py
@@ -143,7 +143,7 @@
     column = lax.rem(blk, n_y)
     ring = sorted(
         [(dz, dy) for dz in range(depth) for dy in range(n_y) if dz + dy],
-        key=lambda at: -(min(at[0], depth - at[0]) + min(at[1], n_y - at[1])),
+        key=lambda at: -(min(at[0], depth - at[0]) + 2 * min(at[1], n_y - at[1])),
     )
 
     def peer(place):
@@ -177,31 +177,23 @@
     rhs_load = pltpu.make_async_copy(rhs_hbm, rhs_ref, load_sem.at[LEVELS])
     panels_load = pltpu.make_async_copy(panels_hbm, panels_ref, load_sem.at[LEVELS + 1])
     maps_load = pltpu.make_async_copy(maps_hbm, maps_ref, load_sem.at[LEVELS + 2])
+    barrier = pltpu.get_barrier_semaphore()
+
+    def greet(target):
+        pl.semaphore_signal(
+            barrier, inc=1, device_id=target, device_id_type=pl.DeviceIdType.MESH
+        )
+
+    for place in ring:
+        greet(device(cube, peer(place)))
+    for member in members(cube, n_cube):
+        greet(device(member, blk))
     diag_loads[0].start()
     rhs_load.start()
     panels_load.start()
     maps_load.start()
     for load in diag_loads[1:]:
         load.start()
-
-    barrier = pltpu.get_barrier_semaphore()
-
-    def greet_blk(step, carry):
-        pl.semaphore_signal(
-            barrier, inc=1, device_id=device(cube, lax.rem(blk + step, n_blk)),
-            device_id_type=pl.DeviceIdType.MESH,
-        )
-        return carry
-
-    def greet_cube(step, carry):
-        pl.semaphore_signal(
-            barrier, inc=1, device_id=device(lax.rem(cube + step, n_cube), blk),
-            device_id_type=pl.DeviceIdType.MESH,
-        )
-        return carry
-
-    lax.fori_loop(1, n_blk, greet_blk, 0)
-    lax.fori_loop(1, n_cube, greet_cube, 0)
 
     def wide_of(level):
         return slice(3 * FOLD * (2**level - 1) * ROWS, 3 * FOLD * (2**(level + 1) - 1) * ROWS)
@@ -431,8 +423,25 @@
                 first(stream, level)
                 second(stream, level)
 
+    def drain_up(level):
+        for stream in streams:
+            wait_for(part.at[stream, level, others], rs_send_sem.at[stream, level])
+            if level + 1 < LEVELS:
+                rest = pl.ds(0, 2 * 2**level - 1)
+                wait_for(spread.at[stream, level, rest], up_send_sem.at[stream, level])
+        if level + 1 < LEVELS:
+            wait_for(facts.at[level, rest], fact_send_sem.at[level])
+
+    def drain_down(level):
+        rest = pl.ds(0, 2**level - 1)
+        for stream in streams:
+            wait_for(gather.at[stream, level, others], ag_send_sem.at[stream, level])
+            for source, sem in ((sums_send, down_send_sem), (rows_send, rows_send_sem)):
+                wait_for(source.at[stream, level - 1, rest], sem.at[stream, level - 1])
+
     for level in range(LEVELS):
         in_turn(climb, enter, level, UP_TURNS[level])
+        drain_up(level)
         if level + 2 < LEVELS:
             combine(level + 1)
         elif level + 2 == LEVELS:
@@ -443,25 +452,13 @@
                 prepare_backward(low)
     for level in reversed(range(LEVELS)):
         in_turn(descend, leave, level, DOWN_TURNS[level])
-        for stream in streams:
-            finish(stream, level)
-
-    for level in range(LEVELS - 1):
-        rest = pl.ds(0, 2 * 2**level - 1)
-        wait_for(facts.at[level, rest], fact_send_sem.at[level])
+        if level:
+            for stream in streams:
+                finish(stream, level)
+            drain_down(level)
+
     for stream in streams:
-        for level in range(LEVELS):
-            wait_for(part.at[stream, level, others], rs_send_sem.at[stream, level])
-            wait_for(gather.at[stream, level, others], ag_send_sem.at[stream, level])
-            if level + 1 < LEVELS:
-                rest = pl.ds(0, 2 * 2**level - 1)
-                wait_for(spread.at[stream, level, rest], up_send_sem.at[stream, level])
-                wait_for(
-                    sums_send.at[stream, level, rest], down_send_sem.at[stream, level]
-                )
-                wait_for(
-                    rows_send.at[stream, level, rest], rows_send_sem.at[stream, level]
-                )
+        wait_for(gather.at[stream, 0, others], ag_send_sem.at[stream, 0])
 
 
 def body(n_cube, n_blk, right_side, diag_inverse, panels, extend_map):
@@ -503,9 +500,9 @@
         + [pltpu.SemaphoreType.DMA((LEVELS - 1,))] * 2
         + [pltpu.SemaphoreType.DMA((LEVELS + 3,))],
         compiler_params=pltpu.CompilerParams(
-            collective_id=0, has_side_effects=True, vmem_limit_bytes=62 * 2**20
+            collective_id=0, has_side_effects=True, vmem_limit_bytes=40 * 2**20
         ),
-    )(rhs, diag_inverse, blocks, maps)
+    )(*[pltpu.with_memory_space_constraint(x, pltpu.HBM) for x in (rhs, diag_inverse, blocks, maps)])
     return result[:, None, None]
 
 

time: 86.6 us -> 84.4 us (0.975)
  Pallas kernels: 85 us -> 83.7 us
    pallas_call x1, Pallas kernels: 85 us -> 83.7 us  [body(): pl.pallas_call(functools.partial(kernel, n_cube, n_blk), out_shape=jax.Sh...]
where the time goes in v6:
time: 84.4 us; the launch traced here: 84.3 us
  Pallas kernels  83.7 us (99%)
    pallas_call x1, Pallas kernels, body(): pl.pallas_call(functools.partial(kernel, n_cube, n_blk), out_shape=jax.Sh...  83.7 us

profile of v6, /device:TPU:1, one launch (start us, length us, event | category | flops | bytes accessed | tf_op | source)
XLA Modules:
  0.0 84.3 jit_solution(16139189515518978478)
XLA Ops:
  0.0 83.7 %shard_map.46 = f32[4,32,64]{2,1,0:T(8,128)S(1)} custom-call(f32[4,32,64]{2,1,0:T(8,128)} %bitcast.7, f32[480,1024]{1,0:T(8,128)} %diag_hbm.1, f32[3,2,16,32]{3,2,1,0:T(8,128)} %bitcast.8, s32[3,2,16]{2,1,0:T(2,128)} %bitcast.9), custom_call_target="tpu_custom_call" | custom-call | tf_op jit(solution)/shard_map/pallas_call | solution.py:473
  83.7 0.6 copy.7

commit v7 on v6

--- a/solution.py
+++ b/solution.py
@@ -146,6 +146,12 @@
         key=lambda at: -(min(at[0], depth - at[0]) + 2 * min(at[1], n_y - at[1])),
     )
 
+    halves = [
+        [dz for dz in range(depth) if (min(dz, depth - dz) >= depth // 4) == far]
+        for far in (True, False)
+    ]
+    halves = [half for half in halves if half]
+
     def peer(place):
         return lax.rem(plane + place[0], depth) * n_y + lax.rem(column + place[1], n_y)
 
@@ -270,7 +276,7 @@
     def wait_for(ref, sem):
         pltpu.make_async_copy(ref, ref, sem).wait()
 
-    def scatter_start(stream, level):
+    def scatter_start(stream, level, distances):
         def step(place):
             to = peer(place)
             pltpu.make_async_remote_copy(
@@ -283,7 +289,8 @@
             ).start()
 
         for place in ring:
-            step(place)
+            if place[0] in distances:
+                step(place)
 
     def gather_start(stream, level):
         def step(place):
@@ -307,13 +314,24 @@
         return pl.ds(stream * COLS, COLS)
 
     def scatter(stream, level, entry):
-        products = dot(forward[:, wide_of(level)], spread_terms(entry))
-        if level:
-            products = base_rows[stream, level - 1] + SCALE * products
-        part[stream, level] = products.reshape(n_blk, SUB, LANES)
-        if level == 0 and stream == 0:
-            pl.semaphore_wait(barrier, n_blk + n_cube - 2)
-        scatter_start(stream, level)
+        terms = spread_terms(entry)
+        slab = n_y * SUB
+        for distances in halves:
+            planes = [lax.rem(plane + dz, depth) for dz in distances]
+            starts = [pl.multiple_of(at * slab, slab) for at in planes]
+            rows = jnp.concatenate(
+                [forward[pl.ds(at, slab), wide_of(level)] for at in starts], axis=0
+            )
+            products = dot(rows, terms)
+            for i, at in enumerate(planes):
+                piece = products[i * slab : (i + 1) * slab]
+                if level:
+                    known = base_rows[stream, level - 1, pl.ds(starts[i], slab)]
+                    piece = known + SCALE * piece
+                part[stream, level, pl.ds(at * n_y, n_y)] = piece.reshape(n_y, SUB, LANES)
+            if level == 0 and stream == 0 and distances is halves[0]:
+                pl.semaphore_wait(barrier, n_blk + n_cube - 2)
+            scatter_start(stream, level, distances)
         rs_recv[stream, level, blk] = part[stream, level, blk]
 
     def climb(stream, level):

time: 84.4 us -> 84.2 us (level)
  no operation moved by 1% of the time
where the time goes in v7:
time: 84.2 us; the launch traced here: 84.1 us
  Pallas kernels  83.4 us (99%)
    pallas_call x1, Pallas kernels, body(): pl.pallas_call(functools.partial(kernel, n_cube, n_blk), out_shape=jax.Sh...  83.4 us

profile of v7, /device:TPU:1, one launch (start us, length us, event | category | flops | bytes accessed | tf_op | source)
XLA Modules:
  0.0 84.1 jit_solution(599922850813806384)
XLA Ops:
  0.0 83.4 %shard_map.46 = f32[4,32,64]{2,1,0:T(8,128)S(1)} custom-call(f32[4,32,64]{2,1,0:T(8,128)} %bitcast.7, f32[480,1024]{1,0:T(8,128)} %diag_hbm.1, f32[3,2,16,32]{3,2,1,0:T(8,128)} %bitcast.8, s32[3,2,16]{2,1,0:T(2,128)} %bitcast.9), custom_call_target="tpu_custom_call" | custom-call | tf_op jit(solution)/shard_map/pallas_call | solution.py:491
  83.4 0.6 copy.7
